TPU v7x, 32 devices: a whole 2x2x4 slice. The times are simulated.
32 devices in a mesh: gx: 2 (over core), gy: 4 (over z), gz: 4 (over y, x).
Axes of the slice: x: 2, y: 2, z: 4, core: 2. Of those that a mesh axis runs over, the one named last changes fastest.
Arguments:
- particles: float32 [28, 65536], P(None, ('gx', 'gy', 'gz')), may hold values from -3 to 3, as said below
- stencil_base: int32 [3, 65536], P(None, ('gx', 'gy', 'gz')), may hold values from 0 to 32, as said below
- weights: float32 [8, 65536], P(None, ('gx', 'gy', 'gz')), may hold values from 0.02 to 0.25
- gradients: float32 [3, 8, 65536], P(None, None, ('gx', 'gy', 'gz')), may hold values from -4 to 4
- counts: int32 [32], P(('gx', 'gy', 'gz')), may hold values from 0 to 8, as said below
Outputs:
- migrated: float32 [28, 98304], P(None, ('gx', 'gy', 'gz'))
- damage: float32 [16, 64, 128], P('gx', 'gy', 'gz')
Inputs may be any that keep to these rules, and one draw needn't show every extreme that they name: `particles`: mass and volume in 0.5 to 2, deformation gradient entries within 0.1 of the identity's, damage in 0 to 0.5, history in 0.05 to 1. `stencil_base`: row 0 lies in 0 to 8, row 1 in 0 to 16, row 2 in 0 to 32. `counts`: some device hands exactly 8 bins.
All inputs are finite; a program needn't handle non-finite values.
Results may differ from a plain program's by a relative error of at most 0.0003.
Values sent between devices are 32-bit elements; how exact they have to be, the bound alone decides.
A program may use at most 64 MiB of HBM per device.

v0:
```python
import jax
import jax.numpy as jnp
from jax import lax
from jax.sharding import PartitionSpec as P

CX = 8
CY = 16
CZ = 32
NBIN = 16
BIN = 128
SUBSTEPS = 4
MOST = 8


time_step = 0.1
relax_rate = 0.2
length_sq = 0.6
shear_mod = 1.0
bulk_coef = 1.5
mass_floor = 0.5


def with_halo(value, sides, width):
    for axis, dim in sides:
        count, length = (lax.axis_size(axis), value.shape[dim])
        up = [(i, (i + 1) % count) for i in range(count - 1)]
        down = [(j, i) for i, j in up]
        last = lax.slice_in_dim(value, length - width, length, axis=dim)
        leading = lax.slice_in_dim(value, 0, width, axis=dim)
        before = lax.ppermute(last, axis, up)
        after = lax.ppermute(leading, axis, down)
        value = jnp.concatenate([before, value, after], axis=dim)
    return value


def passed_along(value, axis, by):
    count = lax.axis_size(axis)
    return lax.ppermute(value, axis, [(i, (i + by) % count) for i in range(count)])


def corner_offsets(corner):
    return (corner >> 2 & 1, corner >> 1 & 1, corner & 1)


def node_terms(particles, weights, gradients, corner):
    volume = particles[1]
    velocity = particles[2:5]
    stress = particles[14:23].reshape(3, 3, -1)
    share = particles[0] * weights[corner]
    slope = gradients[:, corner]
    force = -volume[None] * jnp.sum(stress * slope[None], axis=1)
    return jnp.concatenate(
        [
            share[None],
            share[None] * velocity,
            force,
            (share * particles[23])[None],
            (share * particles[24])[None],
        ],
        axis=0,
    )


def relax(padded, drive):
    centre = padded[1:-1, 1:-1, 1:-1]
    laplace = (
        padded[2:, 1:-1, 1:-1]
        + padded[:-2, 1:-1, 1:-1]
        + padded[1:-1, 2:, 1:-1]
        + padded[1:-1, :-2, 1:-1]
        + padded[1:-1, 1:-1, 2:]
        + padded[1:-1, 1:-1, :-2]
        - 6.0 * centre
    )
    return centre + relax_rate * (length_sq * laplace - centre + 2.0 * (1.0 - centre) * drive)


def advance(particles, near_velocity, near_damage, weights, gradients):
    moved = [jnp.sum(weights * near_velocity[i], axis=0) for i in range(3)]
    velgrad = [
        [jnp.sum(near_velocity[i] * gradients[j], axis=0) for j in range(3)] for i in range(3)
    ]
    damage_node = jnp.sum(weights * near_damage, axis=0)
    deform = [[particles[5 + 3 * i + j] for j in range(3)] for i in range(3)]
    stretch = [
        [(1.0 if i == j else 0.0) + time_step * velgrad[i][j] for j in range(3)] for i in range(3)
    ]
    mapped = [
        [
            stretch[i][0] * deform[0][j]
            + stretch[i][1] * deform[1][j]
            + stretch[i][2] * deform[2][j]
            for j in range(3)
        ]
        for i in range(3)
    ]
    jacobian = (
        mapped[0][0] * (mapped[1][1] * mapped[2][2] - mapped[1][2] * mapped[2][1])
        - mapped[0][1] * (mapped[1][0] * mapped[2][2] - mapped[1][2] * mapped[2][0])
        + mapped[0][2] * (mapped[1][0] * mapped[2][1] - mapped[1][1] * mapped[2][0])
    )
    left = [
        [
            mapped[i][0] * mapped[j][0] + mapped[i][1] * mapped[j][1] + mapped[i][2] * mapped[j][2]
            for j in range(3)
        ]
        for i in range(3)
    ]
    damaged = jnp.maximum(particles[23], damage_node)
    degrade = (1.0 - damaged) ** 2
    rows_out = []
    for i in range(3):
        for j in range(3):
            term = shear_mod * (left[i][j] - (1.0 if i == j else 0.0))
            if i == j:
                term = term + bulk_coef * (jacobian - 1.0)
            rows_out.append(degrade * term)
    energy = (
        0.5 * shear_mod * (left[0][0] + left[1][1] + left[2][2] - 3.0)
        + 0.5 * bulk_coef * (jacobian - 1.0) ** 2
    )
    history = jnp.maximum(particles[24], energy)
    position = particles[25:28] + time_step * jnp.stack(moved)
    flat_mapped = jnp.stack([mapped[i][j] for i in range(3) for j in range(3)])
    return jnp.concatenate(
        [
            particles[0:2],
            jnp.stack(moved),
            flat_mapped,
            jnp.stack(rows_out),
            damaged[None],
            history[None],
            position,
        ],
        axis=0,
    )


def fold_rims(array, dim):
    size = array.shape[dim]
    inner = lax.slice_in_dim(array, 2, size - 2, axis=dim)
    lower = lax.slice_in_dim(array, 0, 1, axis=dim)
    upper = lax.slice_in_dim(array, size - 1, size, axis=dim)
    widths_low = [(0, 0)] * array.ndim
    widths_high = [(0, 0)] * array.ndim
    widths_low[dim] = (0, size - 5)
    widths_high[dim] = (size - 5, 0)
    return inner + jnp.pad(lower, widths_low) + jnp.pad(upper, widths_high)


def inside_line(index, devices, cells, margin):
    position = index * cells + jnp.arange(cells + 2 * margin, dtype=jnp.int32) - margin
    return ((position >= 0) & (position < devices * cells)).astype(jnp.float32)


def per_device(particles, stencil_base, weights, gradients, counts):
    span_x = CX + 2
    span_y = CY + 2
    span_z = CZ + 2
    count = particles.shape[1]
    flats = []
    terms = []
    for corner in range(8):
        offset_x, offset_y, offset_z = corner_offsets(corner)
        flat_index = (
            ((stencil_base[0] + offset_x) * span_y + stencil_base[1] + offset_y) * span_z
            + stencil_base[2]
            + offset_z
        )
        flats.append(flat_index)
        terms.append(node_terms(particles, weights, gradients, corner))
    all_index = jnp.concatenate(flats)
    grid_sum = (
        jnp.zeros((9, span_x * span_y * span_z), jnp.float32)
        .at[:, all_index]
        .add(jnp.concatenate(terms, axis=1))
    )
    extended = grid_sum.reshape(9, span_x, span_y, span_z)
    haloed = with_halo(extended, (("gx", 1), ("gy", 2), ("gz", 3)), 1)
    owned = fold_rims(fold_rims(fold_rims(haloed, 1), 2), 3)
    masses = jnp.maximum(owned[0], mass_floor)
    velocity = (owned[1:4] + time_step * owned[4:7]) / masses[None]
    damage = owned[7] / masses
    drive = owned[8] / masses
    deep = with_halo(jnp.stack([damage, drive]), (("gx", 1), ("gy", 2), ("gz", 3)), SUBSTEPS)
    line_x = inside_line(lax.axis_index("gx"), lax.axis_size("gx"), CX, SUBSTEPS)
    line_y = inside_line(lax.axis_index("gy"), lax.axis_size("gy"), CY, SUBSTEPS)
    line_z = inside_line(lax.axis_index("gz"), lax.axis_size("gz"), CZ, SUBSTEPS)
    inside = line_x[:, None, None] * line_y[None, :, None] * line_z[None, None, :]
    current = deep[0]
    for step in range(SUBSTEPS):
        trim = step + 1
        local_drive = deep[1][trim:-trim, trim:-trim, trim:-trim]
        current = relax(current, local_drive) * inside[trim:-trim, trim:-trim, trim:-trim]
    damage = current
    fields = jnp.concatenate([velocity, damage[None]], axis=0)
    near_all = with_halo(fields, (("gx", 1), ("gy", 2), ("gz", 3)), 1).reshape(4, -1)
    near = near_all[:, all_index].reshape(4, 8, count)
    updated = advance(particles, near[0:3], near[3], weights, gradients)
    tail = updated[:, (NBIN - MOST) * BIN :]
    sent_count = counts.astype(jnp.float32)
    recv_tail, recv_count = passed_along((tail, sent_count), "gz", 1)
    prior = recv_count[0].astype(jnp.int32)
    own_count = counts[0]
    buffer_all = jnp.concatenate(
        [recv_tail, updated, jnp.zeros((updated.shape[0], MOST * BIN), updated.dtype)], axis=1
    )
    start = (MOST - prior) * BIN
    window = lax.dynamic_slice_in_dim(buffer_all, start, (NBIN + MOST) * BIN, 1)
    live = (NBIN - own_count + prior) * BIN
    slot = jnp.arange((NBIN + MOST) * BIN, dtype=jnp.int32)
    migrated = jnp.where(slot[None, :] < live, window, jnp.zeros_like(window))
    return (migrated, damage)


def solution(mesh):
    return jax.shard_map(
        per_device,
        mesh=mesh,
        in_specs=(
            P(None, ("gx", "gy", "gz")),
            P(None, ("gx", "gy", "gz")),
            P(None, ("gx", "gy", "gz")),
            P(None, None, ("gx", "gy", "gz")),
            P(("gx", "gy", "gz")),
        ),
        out_specs=(P(None, ("gx", "gy", "gz")), P("gx", "gy", "gz")),
        check_vma=False,
    )
```

profile of v0, /device:TPU:0, one launch (start us, length us, event | category | flops | bytes accessed | tf_op | source)
XLA Modules:
  0.0 303.8 jit_solution(7041920982947961368)
XLA Ops:
  0.6 1.0 slice.445
  1.6 1.2 slice_multiply_fusion.17
  2.9 1.0 slice_multiply_fusion.23
  3.8 2.0 fusion.59
  7.6 4.7 %copy.15 = f32[16384,9]{1,0:T(8,128)} copy(f32[16384,9]{0,1:T(8,128)S(1)} %bitcast.101) | data formatting | bytes 1179648 | tf_op jit(solution)/shard_map/concatenate | solution.py:176
  13.2 88.4 %scatter_custom_fusion = f32[9,6120]{0,1:T(8,128)S(1)} fusion(s32[16384]{0:T(1024)S(1)} %bitcast.102, f32[16384,9]{1,0:T(8,128)} %copy.15, f32[]{:T(128)} %constant.36.clone.1), kind=kCustom, calls=%fused_computation.6 | custom fusion | flops 147456 | bytes 220832 | tf_op jit(solution)/shard_map/scatter-add | solution.py:176
  101.6 1.5 copy.16
  103.7 2.4 collective-permute-start.1
  106.1 1.3 collective-permute-start.2
  107.5 1.8 collective-permute-done.2
  109.4 4.3 %collective-permute-start.3 = (f32[9,12,1,34]{3,2,1,0:T(1,128)S(1)}, f32[9,12,1,34]{3,2,1,0:T(1,128)S(1)}, u32[]{:S(2)}, u32[]{:S(2)}) collective-permute-start(f32[9,12,1,34]{3,2,1,0:T(1,128)S(1)} %get-tuple-element.66), channel_id=1, source_target_pairs={{0,4},{4,8},{8,12},{1,5},{5,9},{9,13},{2,6},{6,10},{10,14},{3,7},{... | collective-permute-start | bytes 44072 | tf_op jit(solution)/shard_map/ppermute | solution.py:30
  113.7 1.3 collective-permute-start.4
  115.5 4.3 %collective-permute-done.4 = f32[9,12,1,34]{3,2,1,0:T(1,128)S(1)} collective-permute-done((f32[9,12,1,34]{3,2,1,0:T(1,128)S(1)}, f32[9,12,1,34]{3,2,1,0:T(1,128)S(1)}, u32[]{:S(2)}, u32[]{:S(2)}) %collective-permute-start.4) | collective-permute-done | bytes 14720 | tf_op jit(solution)/shard_map/ppermute | solution.py:31
  120.1 1.5 fusion.54
  121.6 2.0 copy.17
  123.6 3.4 %collective-permute-start.5 = (f32[9,12,20,1]{2,3,1,0:T(1,128)S(1)}, f32[9,12,20,1]{2,3,1,0:T(1,128)S(1)}, u32[]{:S(2)}, u32[]{:S(2)}) collective-permute-start(f32[9,12,20,1]{2,3,1,0:T(1,128)S(1)} %copy.17), channel_id=1, source_target_pairs={{0,1},{1,2},{2,3},{4,5},{5,6},{6,7},{8,9},{9,10},{10,11},{12,13},{... | collective-permute-start | bytes 25928 | tf_op jit(solution)/shard_map/ppermute | solution.py:30
  127.8 1.3 collective-permute-start.6
  129.1 0.8 copy.19
  129.9 3.9 %collective-permute-done.6 = f32[9,12,20,1]{2,3,1,0:T(1,128)S(1)} collective-permute-done((f32[9,12,20,1]{2,3,1,0:T(1,128)S(1)}, f32[9,12,20,1]{2,3,1,0:T(1,128)S(1)}, u32[]{:S(2)}, u32[]{:S(2)}) %collective-permute-start.6) | collective-permute-done | bytes 8672 | tf_op jit(solution)/shard_map/ppermute | solution.py:31
  133.8 1.8 copy.20
  135.6 2.4 pad_maximum_fusion.1
  139.8 1.3 collective-permute-start.7
  141.1 1.3 collective-permute-start.8
  142.4 1.8 collective-permute-done.8
  144.3 1.3 collective-permute-start.10
  145.6 4.5 %collective-permute-start.9 = (f32[2,16,4,32]{3,2,1,0:T(4,128)S(1)}, f32[2,16,4,32]{3,2,1,0:T(4,128)S(1)}, u32[]{:S(2)}, u32[]{:S(2)}) collective-permute-start(f32[2,16,4,32]{3,2,1,0:T(4,128)S(1)} %get-tuple-element.95), channel_id=1, source_target_pairs={{0,4},{4,8},{8,12},{1,5},{5,9},{9,13},{2,6},{6,10},{10,14},{3,7},{... | collective-permute-start | bytes 49160 | tf_op jit(solution)/shard_map/ppermute | solution.py:30
  150.5 1.6 collective-permute-done.9
  152.3 4.3 %collective-permute-start.11 = (f32[2,16,24,4]{3,2,1,0:T(8,128)S(1)}, f32[2,16,24,4]{3,2,1,0:T(8,128)S(1)}, u32[]{:S(2)}, u32[]{:S(2)}) collective-permute-start(f32[2,16,24,4]{3,2,1,0:T(8,128)S(1)} %get-tuple-element.77), channel_id=1, source_target_pairs={{0,1},{1,2},{2,3},{4,5},{5,6},{6,7},{8,9},{9,10},{10,11},{12,13},{... | collective-permute-start | bytes 36872 | tf_op jit(solution)/shard_map/ppermute | solution.py:30
  156.6 1.5 collective-permute-start.12
  158.2 6.0 %collective-permute-done.11 = f32[2,16,24,4]{3,2,1,0:T(8,128)S(1)} collective-permute-done((f32[2,16,24,4]{3,2,1,0:T(8,128)S(1)}, f32[2,16,24,4]{3,2,1,0:T(8,128)S(1)}, u32[]{:S(2)}, u32[]{:S(2)}) %collective-permute-start.11) | collective-permute-done | bytes 12320 | tf_op jit(solution)/shard_map/ppermute | solution.py:30
  164.2 9.5 %collective-permute-done.12 = f32[2,16,24,4]{3,2,1,0:T(8,128)S(1)} collective-permute-done((f32[2,16,24,4]{3,2,1,0:T(8,128)S(1)}, f32[2,16,24,4]{3,2,1,0:T(8,128)S(1)}, u32[]{:S(2)}, u32[]{:S(2)}) %collective-permute-start.12) | collective-permute-done | bytes 12320 | tf_op jit(solution)/shard_map/ppermute | solution.py:31
  175.4 1.3 collective-permute-start.13
  176.7 1.3 collective-permute-start.14
  178.0 1.8 collective-permute-done.14
  179.9 4.0 %collective-permute-start.15 = (f32[4,10,1,32]{3,2,1,0:T(1,128)S(1)}, f32[4,10,1,32]{3,2,1,0:T(1,128)S(1)}, u32[]{:S(2)}, u32[]{:S(2)}) collective-permute-start(f32[4,10,1,32]{3,2,1,0:T(1,128)S(1)} %get-tuple-element.79), channel_id=1, source_target_pairs={{0,4},{4,8},{8,12},{1,5},{5,9},{9,13},{2,6},{6,10},{10,14},{3,7},{... | collective-permute-start | bytes 15368 | tf_op jit(solution)/shard_map/ppermute | solution.py:30
  183.8 1.3 collective-permute-start.16
  185.8 1.6 collective-permute-start
  187.4 2.1 collective-permute-done.16
  189.8 2.2 collective-permute-start.17
  192.0 1.3 collective-permute-start.18
  193.9 7.4 %collective-permute-done.17 = f32[4,10,18,1]{3,2,1,0:T(8,128)S(1)} collective-permute-done((f32[4,10,18,1]{3,2,1,0:T(8,128)S(1)}, f32[4,10,18,1]{3,2,1,0:T(8,128)S(1)}, u32[]{:S(2)}, u32[]{:S(2)}) %collective-permute-start.17) | collective-permute-done | bytes 2912 | tf_op jit(solution)/shard_map/ppermute | solution.py:30
  201.4 11.3 %collective-permute-done.18 = f32[4,10,18,1]{3,2,1,0:T(8,128)S(1)} collective-permute-done((f32[4,10,18,1]{3,2,1,0:T(8,128)S(1)}, f32[4,10,18,1]{3,2,1,0:T(8,128)S(1)}, u32[]{:S(2)}, u32[]{:S(2)}) %collective-permute-start.18) | collective-permute-done | bytes 2912 | tf_op jit(solution)/shard_map/ppermute | solution.py:31
  213.3 1.6 copy.21
  214.9 54.4 %gather_fusion = f32[16384,4]{1,0:T(8,128)} fusion(f32[4,6120]{0,1:T(8,128)S(1)} %copy.21, s32[16384]{0:T(1024)S(1)} %broadcast_clamp_fusion), kind=kCustom, calls=%fused_computation | custom fusion | bytes 589824 | tf_op jit(solution)/shard_map/gather | solution.py:198
  269.3 26.0 %slice_reduce_fusion = (f32[16384]{0:T(1024)S(1)}, f32[16384]{0:T(1024)S(1)}, f32[16384]{0:T(1024)S(1)}, f32[16384]{0:T(1024)S(1)}) fusion(f32[4,16384]{0,1:T(8,128)} %bitcast.96), kind=kLoop, calls=%fused_computation.2 | loop fusion | bytes 524288 | tf_op jit(solution)/shard_map/slice | solution.py:199
  297.0 2.4 collective-permute-start.19
  299.5 3.5 %collective-permute-done.19 = f32[28,1024]{1,0:T(8,128)S(1)} collective-permute-done((f32[28,1024]{1,0:T(8,128)S(1)}, f32[28,1024]{1,0:T(8,128)S(1)}, u32[]{:S(2)}, u32[]{:S(2)}) %collective-permute-start.19) | collective-permute-done | bytes 114720 | tf_op jit(solution)/shard_map/ppermute | solution.py:38
  302.9 0.8 fusion.15
  (128 shorter events, 11.6 us)
Async XLA Ops:
  0.6 5.4 %copy-start.4 = (f32[28,2048]{1,0:T(8,128)S(1)}, f32[28,2048]{1,0:T(8,128)}, u32[]{:S(2)}) copy-start(f32[28,2048]{1,0:T(8,128)} %param.5) | copy-start | bytes 688132
  7.5 4.7 %copy-start.3 = (s32[3,2048]{1,0:T(4,128)S(1)}, s32[3,2048]{1,0:T(4,128)}, u32[]{:S(2)}) copy-start(s32[3,2048]{1,0:T(4,128)} %param.6) | copy-start | bytes 73732
  12.6 0.6 copy-start.7
  103.7 3.7 %collective-permute-start.1 = (f32[9,1,18,34]{3,2,1,0:T(8,128)S(1)}, f32[9,1,18,34]{3,2,1,0:T(8,128)S(1)}, u32[]{:S(2)}, u32[]{:S(2)}) collective-permute-start(f32[9,1,18,34]{3,2,1,0:T(8,128)S(1)} %get-tuple-element.69), channel_id=1, source_target_pairs={{0,16},{1,17},{2,18},{3,19},{4,20},{5,21},{6,22},{7,23},{8,24},{9,... | collective-permute-start | bytes 66104 | tf_op jit(solution)/shard_map/ppermute | solution.py:30
  106.1 3.2 %collective-permute-start.2 = (f32[9,1,18,34]{3,2,1,0:T(8,128)S(1)}, f32[9,1,18,34]{3,2,1,0:T(8,128)S(1)}, u32[]{:S(2)}, u32[]{:S(2)}) collective-permute-start(f32[9,1,18,34]{3,2,1,0:T(8,128)S(1)} %get-tuple-element.68), channel_id=1, source_target_pairs={{16,0},{17,1},{18,2},{19,3},{20,4},{21,5},{22,6},{23,7},{24,8},{25... | collective-permute-start | bytes 66104 | tf_op jit(solution)/shard_map/ppermute | solution.py:31
  109.4 6.1 %collective-permute-start.3 = (f32[9,12,1,34]{3,2,1,0:T(1,128)S(1)}, f32[9,12,1,34]{3,2,1,0:T(1,128)S(1)}, u32[]{:S(2)}, u32[]{:S(2)}) collective-permute-start(f32[9,12,1,34]{3,2,1,0:T(1,128)S(1)} %get-tuple-element.66), channel_id=1, source_target_pairs={{0,4},{4,8},{8,12},{1,5},{5,9},{9,13},{2,6},{6,10},{10,14},{3,7},{... | collective-permute-start | bytes 44072 | tf_op jit(solution)/shard_map/ppermute | solution.py:30
  113.7 6.0 %collective-permute-start.4 = (f32[9,12,1,34]{3,2,1,0:T(1,128)S(1)}, f32[9,12,1,34]{3,2,1,0:T(1,128)S(1)}, u32[]{:S(2)}, u32[]{:S(2)}) collective-permute-start(f32[9,12,1,34]{3,2,1,0:T(1,128)S(1)} %get-tuple-element.67), channel_id=1, source_target_pairs={{4,0},{8,4},{12,8},{5,1},{9,5},{13,9},{6,2},{10,6},{14,10},{7,3},{... | collective-permute-start | bytes 44072 | tf_op jit(solution)/shard_map/ppermute | solution.py:31
  123.6 5.5 %collective-permute-start.5 = (f32[9,12,20,1]{2,3,1,0:T(1,128)S(1)}, f32[9,12,20,1]{2,3,1,0:T(1,128)S(1)}, u32[]{:S(2)}, u32[]{:S(2)}) collective-permute-start(f32[9,12,20,1]{2,3,1,0:T(1,128)S(1)} %copy.17), channel_id=1, source_target_pairs={{0,1},{1,2},{2,3},{4,5},{5,6},{6,7},{8,9},{9,10},{10,11},{12,13},{... | collective-permute-start | bytes 25928 | tf_op jit(solution)/shard_map/ppermute | solution.py:30
  127.8 6.0 %collective-permute-start.6 = (f32[9,12,20,1]{2,3,1,0:T(1,128)S(1)}, f32[9,12,20,1]{2,3,1,0:T(1,128)S(1)}, u32[]{:S(2)}, u32[]{:S(2)}) collective-permute-start(f32[9,12,20,1]{2,3,1,0:T(1,128)S(1)} %copy.18), channel_id=1, source_target_pairs={{1,0},{2,1},{3,2},{5,4},{6,5},{7,6},{9,8},{10,9},{11,10},{13,12},{... | collective-permute-start | bytes 25928 | tf_op jit(solution)/shard_map/ppermute | solution.py:31
  135.6 2.4 copy-start
  135.6 2.4 copy-start.10
  138.1 0.7 copy-start.11
  138.7 0.7 copy-start.9
  139.8 2.6 collective-permute-start.7
  141.1 3.1 %collective-permute-start.8 = (f32[2,4,16,32]{3,2,1,0:T(8,128)S(1)}, f32[2,4,16,32]{3,2,1,0:T(8,128)S(1)}, u32[]{:S(2)}, u32[]{:S(2)}) collective-permute-start(f32[2,4,16,32]{3,2,1,0:T(8,128)S(1)} %get-tuple-element.123), channel_id=1, source_target_pairs={{16,0},{17,1},{18,2},{19,3},{20,4},{21,5},{22,6},{23,7},{24,8},{25... | collective-permute-start | bytes 49160 | tf_op jit(solution)/shard_map/ppermute | solution.py:31
  144.3 6.2 %collective-permute-start.10 = (f32[2,16,4,32]{3,2,1,0:T(4,128)S(1)}, f32[2,16,4,32]{3,2,1,0:T(4,128)S(1)}, u32[]{:S(2)}, u32[]{:S(2)}) collective-permute-start(f32[2,16,4,32]{3,2,1,0:T(4,128)S(1)} %get-tuple-element.96), channel_id=1, source_target_pairs={{4,0},{8,4},{12,8},{5,1},{9,5},{13,9},{6,2},{10,6},{14,10},{7,3},{... | collective-permute-start | bytes 49160 | tf_op jit(solution)/shard_map/ppermute | solution.py:31
  145.6 6.4 %collective-permute-start.9 = (f32[2,16,4,32]{3,2,1,0:T(4,128)S(1)}, f32[2,16,4,32]{3,2,1,0:T(4,128)S(1)}, u32[]{:S(2)}, u32[]{:S(2)}) collective-permute-start(f32[2,16,4,32]{3,2,1,0:T(4,128)S(1)} %get-tuple-element.95), channel_id=1, source_target_pairs={{0,4},{4,8},{8,12},{1,5},{5,9},{9,13},{2,6},{6,10},{10,14},{3,7},{... | collective-permute-start | bytes 49160 | tf_op jit(solution)/shard_map/ppermute | solution.py:30
  152.3 11.8 %collective-permute-start.11 = (f32[2,16,24,4]{3,2,1,0:T(8,128)S(1)}, f32[2,16,24,4]{3,2,1,0:T(8,128)S(1)}, u32[]{:S(2)}, u32[]{:S(2)}) collective-permute-start(f32[2,16,24,4]{3,2,1,0:T(8,128)S(1)} %get-tuple-element.77), channel_id=1, source_target_pairs={{0,1},{1,2},{2,3},{4,5},{5,6},{6,7},{8,9},{9,10},{10,11},{12,13},{... | collective-permute-start | bytes 36872 | tf_op jit(solution)/shard_map/ppermute | solution.py:30
  156.6 17.0 %collective-permute-start.12 = (f32[2,16,24,4]{3,2,1,0:T(8,128)S(1)}, f32[2,16,24,4]{3,2,1,0:T(8,128)S(1)}, u32[]{:S(2)}, u32[]{:S(2)}) collective-permute-start(f32[2,16,24,4]{3,2,1,0:T(8,128)S(1)} %get-tuple-element.78), channel_id=1, source_target_pairs={{1,0},{2,1},{3,2},{5,4},{6,5},{7,6},{9,8},{10,9},{11,10},{13,12},{... | collective-permute-start | bytes 36872 | tf_op jit(solution)/shard_map/ppermute | solution.py:31
  175.4 37.3 %copy-start.1 = (f32[8,16,32]{2,1,0:T(8,128)}, f32[8,16,32]{2,1,0:T(8,128)S(1)}, u32[]{:S(2)}) copy-start(f32[8,16,32]{2,1,0:T(8,128)S(1)} %slice_multiply_fusion.7) | copy-start | bytes 49156
  175.4 2.6 collective-permute-start.13
  176.7 3.1 %collective-permute-start.14 = (f32[4,1,16,32]{3,2,1,0:T(8,128)S(1)}, f32[4,1,16,32]{3,2,1,0:T(8,128)S(1)}, u32[]{:S(2)}, u32[]{:S(2)}) collective-permute-start(f32[4,1,16,32]{3,2,1,0:T(8,128)S(1)} %get-tuple-element.94), channel_id=1, source_target_pairs={{16,0},{17,1},{18,2},{19,3},{20,4},{21,5},{22,6},{23,7},{24,8},{25... | collective-permute-start | bytes 24584 | tf_op jit(solution)/shard_map/ppermute | solution.py:31
  179.9 7.6 %collective-permute-start.15 = (f32[4,10,1,32]{3,2,1,0:T(1,128)S(1)}, f32[4,10,1,32]{3,2,1,0:T(1,128)S(1)}, u32[]{:S(2)}, u32[]{:S(2)}) collective-permute-start(f32[4,10,1,32]{3,2,1,0:T(1,128)S(1)} %get-tuple-element.79), channel_id=1, source_target_pairs={{0,4},{4,8},{8,12},{1,5},{5,9},{9,13},{2,6},{6,10},{10,14},{3,7},{... | collective-permute-start | bytes 15368 | tf_op jit(solution)/shard_map/ppermute | solution.py:30
  183.8 5.7 %collective-permute-start.16 = (f32[4,10,1,32]{3,2,1,0:T(1,128)S(1)}, f32[4,10,1,32]{3,2,1,0:T(1,128)S(1)}, u32[]{:S(2)}, u32[]{:S(2)}) collective-permute-start(f32[4,10,1,32]{3,2,1,0:T(1,128)S(1)} %get-tuple-element.80), channel_id=1, source_target_pairs={{4,0},{8,4},{12,8},{5,1},{9,5},{13,9},{6,2},{10,6},{14,10},{7,3},{... | collective-permute-start | bytes 15368 | tf_op jit(solution)/shard_map/ppermute | solution.py:31
  185.8 7.6 %copy-start.8 = (s32[16384,1]{0,1:T(1,128)S(1)}, s32[16384,1]{0,1:T(1,128)}, u32[]{:S(2)}) copy-start(s32[16384,1]{0,1:T(1,128)} %copy-done.7) | copy-start | bytes 196612
  185.8 7.6 %collective-permute-start = (f32[1]{0:T(128)}, f32[1]{0:T(128)}, u32[]{:S(2)}, u32[]{:S(2)}) collective-permute-start(f32[1]{0:T(128)} %convert_element_type.40), channel_id=1, source_target_pairs={{0,1},{1,2},{2,3},{3,0},{4,5},{5,6},{6,7},{7,4},{8,9},{9,10},{10,1... | collective-permute-start | bytes 20 | tf_op jit(solution)/shard_map/ppermute | solution.py:38
  189.8 11.6 %collective-permute-start.17 = (f32[4,10,18,1]{3,2,1,0:T(8,128)S(1)}, f32[4,10,18,1]{3,2,1,0:T(8,128)S(1)}, u32[]{:S(2)}, u32[]{:S(2)}) collective-permute-start(f32[4,10,18,1]{3,2,1,0:T(8,128)S(1)} %get-tuple-element.73), channel_id=1, source_target_pairs={{0,1},{1,2},{2,3},{4,5},{5,6},{6,7},{8,9},{9,10},{10,11},{12,13},{... | collective-permute-start | bytes 8648 | tf_op jit(solution)/shard_map/ppermute | solution.py:30
  192.0 20.6 %collective-permute-start.18 = (f32[4,10,18,1]{3,2,1,0:T(8,128)S(1)}, f32[4,10,18,1]{3,2,1,0:T(8,128)S(1)}, u32[]{:S(2)}, u32[]{:S(2)}) collective-permute-start(f32[4,10,18,1]{3,2,1,0:T(8,128)S(1)} %get-tuple-element.74), channel_id=1, source_target_pairs={{1,0},{2,1},{3,2},{5,4},{6,5},{7,6},{9,8},{10,9},{11,10},{13,12},{... | collective-permute-start | bytes 8648 | tf_op jit(solution)/shard_map/ppermute | solution.py:31
  269.3 26.1 %copy-start.2 = (f32[3,8,2048]{2,1,0:T(8,128)S(1)}, f32[3,8,2048]{2,1,0:T(8,128)}, u32[]{:S(2)}) copy-start(f32[3,8,2048]{2,1,0:T(8,128)} %param.8) | copy-start | bytes 589828
  269.3 26.1 %copy-start.6 = (f32[8,2048]{1,0:T(8,128)S(1)}, f32[8,2048]{1,0:T(8,128)}, u32[]{:S(2)}) copy-start(f32[8,2048]{1,0:T(8,128)} %param.7) | copy-start | bytes 196612
  295.3 1.0 copy-start.5
  295.3 1.4 slice-start
  297.0 5.9 %collective-permute-start.19 = (f32[28,1024]{1,0:T(8,128)S(1)}, f32[28,1024]{1,0:T(8,128)S(1)}, u32[]{:S(2)}, u32[]{:S(2)}) collective-permute-start(f32[28,1024]{1,0:T(8,128)S(1)} %slice.620), channel_id=1, source_target_pairs={{0,1},{1,2},{2,3},{3,0},{4,5},{5,6},{6,7},{7,4},{8,9},{9,10},{10,1... | collective-permute-start | bytes 344072 | tf_op jit(solution)/shard_map/ppermute | solution.py:38
where the time goes:
time: 305 us; the launch traced here: 304 us
  local copies, waits for them, and re-layouts  103 us (34%)
  other arithmetic  99.2 us (33%)
  waiting for transfers between devices  55.5 us (18%)
  starting transfers between devices  43.5 us (14%)
    scatter-add x1, other arithmetic, per_device(): grid_sum = jnp.zeros((9, span_x * span_y * span_z), jnp.float32).at[:, al...  88.4 us
    gather x1, local copies, waits for them, and re-layouts, per_device(): near = near_all[:, all_index].reshape(4, 8, count)  54.4 us
    ppermute x9, waiting for transfers between devices, with_halo(): after = lax.ppermute(leading, axis, down)  36.5 us
    ppermute x9, starting transfers between devices, with_halo(): before = lax.ppermute(last, axis, up)  27.7 us
    slice x1, local copies, waits for them, and re-layouts, per_device(): updated = advance(particles, near[0:3], near[3], weights, gradients)  26 us
    ppermute x9, waiting for transfers between devices, with_halo(): before = lax.ppermute(last, axis, up)  15.5 us
    ppermute x9, starting transfers between devices, with_halo(): after = lax.ppermute(leading, axis, down)  11.8 us
  transfers between devices with their start and end apart: 20, of which 14 were waited for; matrix products, arithmetic and copies ran while one was open for 1% of the time, Pallas kernels for 0%

commit v1 on v0

v1 whole, which is shorter than its diff:
```python
import functools
import jax
import jax.numpy as jnp
from jax import lax
from jax.experimental import pallas as pl
from jax.experimental.pallas import tpu as pltpu
from jax.sharding import PartitionSpec as P

CX = 8
CY = 16
CZ = 32
NBIN = 16
BIN = 128
SUBSTEPS = 4
MOST = 8

time_step = 0.1
relax_rate = 0.2
length_sq = 0.6
shear_mod = 1.0
bulk_coef = 1.5
mass_floor = 0.5

MESH = pl.DeviceIdType.MESH


def up_to(value, unit):
    return (value + unit - 1) // unit * unit


H = SUBSTEPS + 1
SX, SY, SZ = CX + 2 * H, CY + 2 * H, CZ + 2 * H
LW = up_to(SY * SZ, 128)
NB = up_to(CY * SZ + CZ + 1, 128)
OFF = (H - 1) * SZ + H - 1
RD = up_to(SX, 8)
RV = up_to(CX + 2, 8)
XA, XB = (H - 1) * SZ // 128 * 128, up_to((H + 1 + CY) * SZ, 128)
KEEP = H + 1
XROWS = 3 * KEEP + 6
YW = up_to(KEEP * SZ, 128)
YROWS = 3 * RD + 3 * RV // 2
DT, VT = 3 * RD // 8, 3 * RV // 8
SLOTS = SZ // KEEP
PER = KEEP // 2
ZSLOTS = DT + (VT + PER - 1) // PER
ZT = (ZSLOTS + SLOTS - 1) // SLOTS
TAIL = MOST * BIN


def split(value):
    high = value.astype(jnp.bfloat16)
    low = (value - high.astype(jnp.float32)).astype(jnp.bfloat16)
    return high, low


def take(ref, lane0, width):
    a = lane0 // 128 * 128
    span = up_to(lane0 - a + width, 128)
    value = ref[:, a : a + span]
    shift = (span - (lane0 - a)) % span
    if shift:
        value = pltpu.roll(value, shift, 1)
    value = value[:, : up_to(width, 128)]
    lane = lax.broadcasted_iota(jnp.int32, value.shape, 1)
    return jnp.where(lane < width, value, 0.0)


def put_add(ref, lane0, width, value):
    a = lane0 // 128 * 128
    span = max(up_to(lane0 - a + width, 128), value.shape[1])
    extra = span - value.shape[1]
    if extra:
        value = jnp.concatenate([value, jnp.zeros((value.shape[0], extra), jnp.float32)], axis=1)
    if lane0 - a:
        value = pltpu.roll(value, lane0 - a, 1)
    ref[:, a : a + span] += value


def make_onehot(base_ref, hot):
    flat = base_ref[1:2, :] * SZ + base_ref[2:3, :]
    for r in range(0, NB, 128):
        row = lax.broadcasted_iota(jnp.int32, (128, flat.shape[1]), 0) + r
        hot[r : r + 128, :] = (row == flat).astype(jnp.float32).astype(jnp.bfloat16)


def scatter(part, base_ref, weight, slope, hot, coef, left, nodes, dref, vref, xs_low, xs_high):
    count = part.shape[1]
    mass = part[0:1, :]
    scale = -time_step * part[1:2, :]
    coef[...] = jnp.zeros_like(coef)
    coef[0:1, :] = mass
    coef[1:2, :] = mass * part[23:24, :]
    coef[2:3, :] = mass * part[24:25, :]
    coef[3:6, :] = mass * part[2:5, :]
    for j in range(3):
        for i in range(3):
            coef[8 + 8 * j + 3 + i : 8 + 8 * j + 4 + i, :] = scale * part[14 + 3 * i + j : 15 + 3 * i + j, :]
    bx = jnp.broadcast_to(base_ref[0:1, :], (8, count))
    for bc in range(4):
        pair = []
        for a in range(2):
            k = 4 * a + bc
            term = weight[k : k + 1, :] * coef[0:8, :]
            for j in range(3):
                term = term + slope[8 * j + k : 8 * j + k + 1, :] * coef[8 + 8 * j : 16 + 8 * j, :]
            high = term.astype(jnp.bfloat16).astype(jnp.float32)
            pair.append((high, term - high))
        for x in range(CX + 2):
            for s in range(2):
                row = x * 64 + s * 32 + bc * 8
                value = jnp.where(bx == x, pair[0][s], jnp.where(bx == x - 1, pair[1][s], 0.0))
                left[row : row + 8, :] = value.astype(jnp.bfloat16)
    sums = lax.dot_general(left[...], hot[...], (((1,), (1,)), ((), ())), preferred_element_type=jnp.float32)
    sums = sums.reshape(CX + 2, 2, 4, 8, NB)
    sums = sums[:, 0] + sums[:, 1]
    total = None
    for bc in range(4):
        piece = sums[:, bc].reshape((CX + 2) * 8, NB)
        piece = jnp.concatenate([piece, jnp.zeros((piece.shape[0], LW - NB), jnp.float32)], axis=1)
        piece = pltpu.roll(piece, OFF + (bc >> 1) * SZ + (bc & 1), 1)
        total = piece if total is None else total + piece
    for x in range(CX + 2):
        nodes[x] = total[8 * x : 8 * x + 8, :]
    dref[...] = jnp.zeros_like(dref)
    vref[...] = jnp.zeros_like(vref)
    for x in range(CX + 2):
        for c in range(3):
            dref[c * RD + H - 1 + x : c * RD + H + x, :] = nodes[x, c : c + 1, :]
            vref[c * RV + x : c * RV + x + 1, :] = nodes[x, 3 + c : 4 + c, :]
    for c in range(3):
        at = c * RD + H - 1
        xs_high[c * KEEP : (c + 1) * KEEP, :] = dref[at + CX + 2 - KEEP : at + CX + 2, XA:XB]
        xs_low[c * KEEP : (c + 1) * KEEP, :] = dref[at : at + KEEP, XA:XB]
        at = 3 * KEEP + 2 * c
        xs_high[at : at + 2, :] = vref[c * RV + CX : c * RV + CX + 2, XA:XB]
        xs_low[at : at + 2, :] = vref[c * RV : c * RV + 2, XA:XB]


def only(has, value):
    return jnp.where(has, value, jnp.zeros_like(value))


def add_x(dref, vref, from_low, from_high, has_low, has_high, ys_low, ys_high):
    low = only(has_low, from_low[...])
    high = only(has_high, from_high[...])
    for c in range(3):
        dref[c * RD : c * RD + KEEP, XA:XB] += low[c * KEEP : (c + 1) * KEEP]
        dref[c * RD + SX - KEEP : c * RD + SX, XA:XB] += high[c * KEEP : (c + 1) * KEEP]
        at = 3 * KEEP + 2 * c
        vref[c * RV : c * RV + 2, XA:XB] += low[at : at + 2]
        vref[c * RV + CX : c * RV + CX + 2, XA:XB] += high[at : at + 2]
    half = 3 * RV // 2
    for ys, d0, v0 in ((ys_high, CY * SZ, (H - 1 + CY) * SZ), (ys_low, (H - 1) * SZ, (H - 1) * SZ)):
        ys[: 3 * RD, :] = take(dref, d0, KEEP * SZ)
        near = take(vref, v0, 2 * SZ)
        ys[3 * RD :, 0:128] = near[:half]
        ys[3 * RD :, 128:256] = near[half:]


def lane_z():
    lane = lax.broadcasted_iota(jnp.int32, (8, LW), 1).astype(jnp.float32)
    y = jnp.floor((lane + 0.5) * (1.0 / SZ))
    return lane - SZ * y, y


def slot_of(t):
    if t < DT:
        s, sub, width = t, 0, KEEP
    else:
        s, sub, width = DT + (t - DT) // PER, 2 * ((t - DT) % PER), 2
    return s // SLOTS, (s % SLOTS) * KEEP + sub, width


def tile_of(t, dref, vref):
    return dref.at[8 * t : 8 * t + 8] if t < DT else vref.at[8 * (t - DT) : 8 * (t - DT) + 8]


def add_y(dref, vref, from_low, from_high, has_low, has_high, zs_low, zs_high):
    for got, has, d0, v0 in (
        (from_low, has_low, 0, (H - 1) * SZ),
        (from_high, has_high, (SY - KEEP) * SZ, (H - 1 + CY) * SZ),
    ):
        put_add(dref, d0, KEEP * SZ, only(has, got[: 3 * RD, :]))
        near = jnp.concatenate([got[3 * RD :, 0:128], got[3 * RD :, 128:256]], axis=0)
        put_add(vref, v0, 2 * SZ, only(has, near))
    z, _ = lane_z()
    for zs, d0, v0 in ((zs_high, CZ, H - 1 + CZ), (zs_low, H - 1, H - 1)):
        out = [None] * ZT
        for t in range(DT + VT):
            block, at, width = slot_of(t)
            shift = (at - (d0 if t < DT else v0)) % LW
            value = tile_of(t, dref, vref)[...]
            if shift:
                value = pltpu.roll(value, shift, 1)
            value = jnp.where((z >= at) & (z < at + width), value, 0.0)
            out[block] = value if out[block] is None else out[block] + value
        for block in range(ZT):
            zs[8 * block : 8 * block + 8, :] = out[block]


def add_z(dref, vref, from_low, from_high, has_low, has_high):
    z, _ = lane_z()
    for got, has, d0, v0 in (
        (from_low, has_low, 0, H - 1),
        (from_high, has_high, SZ - KEEP, H - 1 + CZ),
    ):
        for t in range(DT + VT):
            block, at, width = slot_of(t)
            value = only(has, got[8 * block : 8 * block + 8, :])
            value = jnp.where((z >= at) & (z < at + width), value, 0.0)
            shift = ((d0 if t < DT else v0) - at) % LW
            if shift:
                value = pltpu.roll(value, shift, 1)
            tile = tile_of(t, dref, vref)
            tile[...] += value


def relax_all(dref, vref, place, nodes_x, nodes_y, nodes_z, wet, fields, field_left, damage_out):
    ix, iy, iz = place
    z, y = lane_z()
    z, y = z[0:1], y[0:1]
    gz = z - H + (iz * CZ).astype(jnp.float32)
    gy = y - H + (iy * CY).astype(jnp.float32)
    flat_in = (gz >= 0) & (gz < nodes_z) & (gy >= 0) & (gy < nodes_y) & (y < SY)
    row = lax.broadcasted_iota(jnp.int32, (RD, 1), 0)
    gx = row - H + ix * CX
    row_in = (gx >= 0) & (gx < nodes_x) & (row < SX)
    inside = row_in.astype(jnp.float32) * flat_in.astype(jnp.float32)
    mass = jnp.maximum(dref[0:RD, :], mass_floor)
    damage = dref[RD : 2 * RD, :] / mass * inside
    drive = dref[2 * RD : 3 * RD, :] / mass
    wet[0:RD, :] = mass
    wet[RD : 2 * RD, :] = inside
    for _ in range(SUBSTEPS):
        ring = (
            pltpu.roll(damage, 1, 0)
            + pltpu.roll(damage, RD - 1, 0)
            + pltpu.roll(damage, SZ, 1)
            + pltpu.roll(damage, LW - SZ, 1)
            + pltpu.roll(damage, 1, 1)
            + pltpu.roll(damage, LW - 1, 1)
        )
        laplace = ring - 6.0 * damage
        damage = (damage + relax_rate * (length_sq * laplace - damage + 2.0 * (1.0 - damage) * drive)) * inside
    wet[2 * RD : 3 * RD, :] = damage
    damage_out[...] = wet[2 * RD + H : 2 * RD + H + CX, :]
    n = CX + 2
    factor = wet[RD + H - 1 : RD + H - 1 + n, :] / wet[H - 1 : H - 1 + n, :]
    fields[...] = jnp.zeros_like(fields)
    for c in range(3):
        fields[c * 16 : c * 16 + n, :] = vref[c * RV : c * RV + n, :] * factor
    fields[48 : 48 + n, :] = wet[2 * RD + H - 1 : 2 * RD + H - 1 + n, :]
    whole = fields[...]
    for bc in range(4):
        moved = pltpu.roll(whole, LW - OFF - (bc >> 1) * SZ - (bc & 1), 1)[:, :NB]
        for f in range(4):
            for x in range(n):
                r = x * 16 + f * 4 + bc
                field_left[r : r + 1, :] = moved[f * 16 + x : f * 16 + x + 1, :]


def advance(part, base_ref, weight, slope, hot, field_left, out, at, count):
    lanes = slice(at, at + count)
    n = CX + 2
    high, low = split(field_left[...])
    got = jnp.dot(high, hot[:, lanes], preferred_element_type=jnp.float32)
    got = got + jnp.dot(low, hot[:, lanes], preferred_element_type=jnp.float32)
    bx = jnp.broadcast_to(base_ref[0:1, lanes], (16, count))
    near = [jnp.zeros((16, count), jnp.float32), jnp.zeros((16, count), jnp.float32)]
    for x in range(n):
        rows = got[16 * x : 16 * x + 16]
        near[0] = jnp.where(bx == x, rows, near[0])
        near[1] = jnp.where(bx == x - 1, rows, near[1])
    w = weight[:, lanes]
    g = [slope[8 * j : 8 * j + 8, lanes] for j in range(3)]
    corner = [jnp.concatenate([near[0][4 * f : 4 * f + 4], near[1][4 * f : 4 * f + 4]], axis=0) for f in range(4)]
    total = lambda v: jnp.sum(v, axis=0, keepdims=True)
    moved = [total(w * corner[i]) for i in range(3)]
    velgrad = [[total(corner[i] * g[j]) for j in range(3)] for i in range(3)]
    damage_node = total(w * corner[3])
    p = lambda r: part[r : r + 1, lanes]
    deform = [[p(5 + 3 * i + j) for j in range(3)] for i in range(3)]
    stretch = [[(1.0 if i == j else 0.0) + time_step * velgrad[i][j] for j in range(3)] for i in range(3)]
    mapped = [
        [stretch[i][0] * deform[0][j] + stretch[i][1] * deform[1][j] + stretch[i][2] * deform[2][j] for j in range(3)]
        for i in range(3)
    ]
    jacobian = (
        mapped[0][0] * (mapped[1][1] * mapped[2][2] - mapped[1][2] * mapped[2][1])
        - mapped[0][1] * (mapped[1][0] * mapped[2][2] - mapped[1][2] * mapped[2][0])
        + mapped[0][2] * (mapped[1][0] * mapped[2][1] - mapped[1][1] * mapped[2][0])
    )
    left = {}
    for i in range(3):
        for j in range(i, 3):
            left[i, j] = mapped[i][0] * mapped[j][0] + mapped[i][1] * mapped[j][1] + mapped[i][2] * mapped[j][2]
            left[j, i] = left[i, j]
    damaged = jnp.maximum(p(23), damage_node)
    degrade = (1.0 - damaged) ** 2
    swell = bulk_coef * (jacobian - 1.0)

    def put(r, value):
        out[r : r + 1, lanes] = value

    out[0:2, lanes] = part[0:2, lanes]
    for i in range(3):
        put(2 + i, moved[i])
        put(25 + i, p(25 + i) + time_step * moved[i])
        for j in range(3):
            put(5 + 3 * i + j, mapped[i][j])
            term = shear_mod * (left[i, j] - (1.0 if i == j else 0.0))
            if i == j:
                term = term + swell
            put(14 + 3 * i + j, degrade * term)
    put(23, damaged)
    energy = 0.5 * shear_mod * (left[0, 0] + left[1, 1] + left[2, 2] - 3.0) + 0.5 * bulk_coef * (jacobian - 1.0) ** 2
    put(24, jnp.maximum(p(24), energy))


def step_kernel(
    sizes, part, base_ref, weight, slope, counts, updated, tail, damage_out,
    hot, coef, left, nodes, dref, vref, wet, fields, field_left,
    sx, rx, sy, ry, sz, rz, give, take_in, send_sem, recv_sem,
):
    names = ("gx", "gy", "gz")
    place = [lax.axis_index(a) for a in names]
    has_low = [i > 0 for i in place]
    has_high = [i < n - 1 for i, n in zip(place, sizes)]
    last = sizes[2]
    following, previous = lax.rem(place[2] + 1, last), lax.rem(place[2] + last - 1, last)
    barrier = pltpu.get_barrier_semaphore()
    waits = 2
    for k in range(2):
        for has, other in ((has_low[k], place[k] - 1), (has_high[k], place[k] + 1)):
            @pl.when(has)
            def _(k=k, other=other):
                pl.semaphore_signal(barrier, inc=1, device_id={names[k]: other}, device_id_type=MESH)
            waits = waits + has.astype(jnp.int32)
    for other in (following, previous):
        pl.semaphore_signal(barrier, inc=1, device_id={"gz": other}, device_id_type=MESH)

    make_onehot(base_ref, hot)
    scatter(part, base_ref, weight, slope, hot, coef, left, nodes, dref, vref, sx.at[0], sx.at[1])
    pl.semaphore_wait(barrier, waits)

    def copies(k, src, dst):
        made = []
        for d, other in ((0, place[k] - 1), (1, place[k] + 1)):
            made.append(pltpu.make_async_remote_copy(
                src_ref=src.at[d], dst_ref=dst.at[1 - d], send_sem=send_sem.at[k, d],
                recv_sem=recv_sem.at[k, 1 - d], device_id={names[k]: other}, device_id_type=MESH))
        return made

    def exchange(k, src, dst):
        made = copies(k, src, dst)
        ahead = ((has_low[k], made[0]), (has_high[k], made[1]))
        for has, copy in ahead:
            @pl.when(has)
            def _(copy=copy):
                copy.start()
        for has, copy in ((has_low[k], made[1]), (has_high[k], made[0])):
            @pl.when(has)
            def _(copy=copy):
                copy.wait_recv()
        for has, copy in ahead:
            @pl.when(has)
            def _(copy=copy):
                copy.wait_send()

    exchange(0, sx, rx)
    add_x(dref, vref, rx.at[0], rx.at[1], has_low[0], has_high[0], sy.at[0], sy.at[1])
    exchange(1, sy, ry)
    add_y(dref, vref, ry.at[0], ry.at[1], has_low[1], has_high[1], sz.at[0], sz.at[1])
    exchange(2, sz, rz)
    add_z(dref, vref, rz.at[0], rz.at[1], has_low[2], has_high[2])
    relax_all(dref, vref, place, sizes[0] * CX, sizes[1] * CY, sizes[2] * CZ, wet, fields, field_left, damage_out)
    count = part.shape[1]
    advance(part, base_ref, weight, slope, hot, field_left, updated, count - TAIL, TAIL)
    give[0:28, :] = updated[:, count - TAIL :]
    give[28:32, :] = jnp.broadcast_to(counts[0].astype(jnp.float32), (4, TAIL))
    pass_on = pltpu.make_async_remote_copy(
        src_ref=give, dst_ref=take_in, send_sem=send_sem.at[3, 0], recv_sem=recv_sem.at[3, 0],
        device_id={"gz": following}, device_id_type=MESH)
    pass_on.start()
    advance(part, base_ref, weight, slope, hot, field_left, updated, 0, count - TAIL)
    pass_on.wait()
    tail[...] = take_in[...]


def per_device(particles, stencil_base, weights, gradients, counts):
    count = particles.shape[1]
    sizes = tuple(lax.axis_size(a) for a in ("gx", "gy", "gz"))
    vmem = pl.BlockSpec(memory_space=pltpu.VMEM)
    f32 = jnp.float32
    updated, tail, flat_damage = pl.pallas_call(
        functools.partial(step_kernel, sizes),
        name="step",
        out_shape=(
            jax.ShapeDtypeStruct((28, count), f32),
            jax.ShapeDtypeStruct((32, TAIL), f32),
            jax.ShapeDtypeStruct((CX, LW), f32),
        ),
        in_specs=[vmem] * 4 + [pl.BlockSpec(memory_space=pltpu.SMEM)],
        out_specs=(vmem,) * 3,
        scratch_shapes=[
            pltpu.VMEM((NB, count), jnp.bfloat16),
            pltpu.VMEM((32, count), f32),
            pltpu.VMEM(((CX + 2) * 64, count), jnp.bfloat16),
            pltpu.VMEM((CX + 2, 8, LW), f32),
            pltpu.VMEM((3 * RD, LW), f32),
            pltpu.VMEM((3 * RV, LW), f32),
            pltpu.VMEM((3 * RD, LW), f32),
            pltpu.VMEM((64, LW), f32),
            pltpu.VMEM(((CX + 2) * 16, NB), f32),
            pltpu.VMEM((2, XROWS, XB - XA), f32),
            pltpu.VMEM((2, XROWS, XB - XA), f32),
            pltpu.VMEM((2, YROWS, YW), f32),
            pltpu.VMEM((2, YROWS, YW), f32),
            pltpu.VMEM((2, 8 * ZT, LW), f32),
            pltpu.VMEM((2, 8 * ZT, LW), f32),
            pltpu.VMEM((32, TAIL), f32),
            pltpu.VMEM((32, TAIL), f32),
            pltpu.SemaphoreType.DMA((4, 2)),
            pltpu.SemaphoreType.DMA((4, 2)),
        ],
        compiler_params=pltpu.CompilerParams(
            collective_id=0, has_side_effects=True, vmem_limit_bytes=60 * 1024 * 1024
        ),
    )(particles, stencil_base, weights, gradients.reshape(24, count), counts)
    damage = flat_damage[:, : SY * SZ].reshape(CX, SY, SZ)[:, H : H + CY, H : H + CZ]
    prior = tail[28, 0].astype(jnp.int32)
    own_count = counts[0]
    buffer_all = jnp.concatenate([tail[:28], updated, jnp.zeros((28, TAIL), f32)], axis=1)
    start = (MOST - prior) * BIN
    window = lax.dynamic_slice_in_dim(buffer_all, start, (NBIN + MOST) * BIN, 1)
    live = (NBIN - own_count + prior) * BIN
    slot = jnp.arange((NBIN + MOST) * BIN, dtype=jnp.int32)
    migrated = jnp.where(slot[None, :] < live, window, jnp.zeros_like(window))
    return (migrated, damage)


def solution(mesh):
    return jax.shard_map(
        per_device,
        mesh=mesh,
        in_specs=(
            P(None, ("gx", "gy", "gz")),
            P(None, ("gx", "gy", "gz")),
            P(None, ("gx", "gy", "gz")),
            P(None, None, ("gx", "gy", "gz")),
            P(("gx", "gy", "gz")),
        ),
        out_specs=(P(None, ("gx", "gy", "gz")), P("gx", "gy", "gz")),
        check_vma=False,
    )
```

time: 305 us -> 31.6 us (0.10)
  local copies, waits for them, and re-layouts: 103 us -> 2.15 us
  other arithmetic: 99.2 us -> 1.82 us
  waiting for transfers between devices: 55.5 us -> 0 us
  starting transfers between devices: 43.5 us -> 0 us
  Pallas kernels: 0 us -> 25.5 us
    scatter-add x1 -> x0, other arithmetic: 88.4 us -> none  [per_device(): grid_sum = jnp.zeros((9, span_x * span_y * span_z), jnp.float32).at[:, al...]
    ppermute x20 -> x0, waiting for transfers between devices: 55.5 us -> none  [the longest x9 36.5 us: with_halo(): after = lax.ppermute(leading, axis, down)]
    gather x1 -> x0, local copies, waits for them, and re-layouts: 54.4 us -> none  [per_device(): near = near_all[:, all_index].reshape(4, 8, count)]
    ppermute x20 -> x0, starting transfers between devices: 43.5 us -> none  [the longest x9 27.7 us: with_halo(): before = lax.ppermute(last, axis, up)]
    slice x15 -> x2, local copies, waits for them, and re-layouts: 34 us -> 1.9 us  [the longest x1 1.19 us: per_device(): prior = tail[28, 0].astype(jnp.int32)]
    pallas_call x0 -> x1, Pallas kernels: none -> 25.5 us  [per_device(): pl.pallas_call(functools.partial(step_kernel, sizes), name='step', out_sh...]
    concatenate x12 -> x0, local copies, waits for them, and re-layouts: 5.68 us -> none  [the longest x2 4.68 us: per_device(): jnp.concatenate(terms, axis=1)]
    mul x19 -> x0, other arithmetic: 4.02 us -> none  [the longest x2 2.18 us: node_terms(): share * particles[24]]
  transfers between devices with their start and end apart: 20 -> 0, of which waited for: 14 -> 0; matrix products, arithmetic and copies ran while one was open for 1% -> 0% of each run, Pallas kernels for 0% -> 0%
where the time goes in v1:
time: 31.6 us; the launch traced here: 31.4 us
  Pallas kernels  25.5 us (81%)
  local copies, waits for them, and re-layouts  2.15 us (7%)
  between operations  1.98 us (6%)
  other arithmetic  1.82 us (6%)
    pallas_call x1, Pallas kernels, per_device(): pl.pallas_call(functools.partial(step_kernel, sizes), name='step', out_sh...  25.5 us
    select_n x1, other arithmetic, per_device(): migrated = jnp.where(slot[None, :] < live, window, jnp.zeros_like(window))  1.81 us
    slice x1, local copies, waits for them, and re-layouts, per_device(): prior = tail[28, 0].astype(jnp.int32)  1.19 us
    slice x1, local copies, waits for them, and re-layouts, per_device(): damage = flat_damage[:, :SY * SZ].reshape(CX, SY, SZ)[:, H:H + CY, H:H + CZ]  0.72 us

profile of v1, /device:TPU:0, one launch (start us, length us, event | category | flops | bytes accessed | tf_op | source)
XLA Modules:
  0.0 31.4 jit_solution(15648078467100096243)
XLA Ops:
  1.3 25.5 %step.1 = (f32[28,2048]{1,0:T(8,128)}, f32[32,1024]{1,0:T(8,128)}, f32[8,1152]{1,0:T(8,128)}) custom-call(f32[28,2048]{1,0:T(8,128)} %part.1, s32[3,2048]{1,0:T(4,128)} %base_ref.1, f32[8,2048]{1,0:T(8,128)} %weight.1, f32[24,2048]{1,0:T(8,128)} %bitcast.5, s32[1]{0:T(128)S(6)} %copy.7.counts), custom_call_target="tpu_custom_call" | custom-call | tf_op jit(solution)/shard_map/step/pallas_call | solution.py:396
  26.7 1.2 %slice.12 = f32[1,1]{1,0:T(1,128)} slice(f32[32,1024]{1,0:T(8,128)} %get-tuple-element.5), slice={[28:29], [0:1]} | slice | bytes 8 | tf_op jit(solution)/shard_map/slice | solution.py:432
  28.6 0.1 pad_dynamic-slice_fusion.2
  28.7 0.0 copy-start
  28.7 1.8 %fusion.2 = f32[28,3072]{1,0:T(8,128)} fusion(s32[]{:T(128)S(6)} %select_n.7, f32[28,1024]{1,0:T(8,128)} %bitcast.6, f32[28,2048]{1,0:T(8,128)} %get-tuple-element.6, f32[3072]{0:T(1024)S(1)} %pad_dynamic-slice_fusion.2, pred[3072]{0:T(1024)(128)(4,1)S(1)} %iota_compare_fusion), kind=kLoop, calls=%fused_computation.4 | loop fusion | flops 258048 | bytes 703492 | tf_op jit(solution)/shard_map/jit(_where)/select_n | solution.py:439
  30.5 0.0 copy-done
  30.5 0.2 reshape.19
  30.7 0.7 %slice.16 = f32[8,16,32]{2,1,0:T(8,128)} slice(f32[8,26,42]{2,1,0:T(8,128)S(1)} %reshape.19), slice={[0:8], [5:21], [5:37]} | slice | bytes 32768 | tf_op jit(solution)/shard_map/slice | solution.py:431
  (2 shorter events, 0.0 us)
Async XLA Ops:
  28.7 1.8 %copy-start = (f32[8,1152]{1,0:T(8,128)S(1)}, f32[8,1152]{1,0:T(8,128)}, u32[]{:S(2)}) copy-start(f32[8,1152]{1,0:T(8,128)} %get-tuple-element.7) | copy-start | bytes 110596

commit v2 on v1

--- a/solution.py
+++ b/solution.py
@@ -34,17 +34,20 @@
 NB = up_to(CY * SZ + CZ + 1, 128)
 OFF = (H - 1) * SZ + H - 1
 RD = up_to(SX, 8)
-RV = up_to(CX + 2, 8)
+DS, VS = SX, CX + 2
+DR, VR = up_to(3 * DS, 8), up_to(3 * VS, 16)
 XA, XB = (H - 1) * SZ // 128 * 128, up_to((H + 1 + CY) * SZ, 128)
 KEEP = H + 1
 XROWS = 3 * KEEP + 6
 YW = up_to(KEEP * SZ, 128)
-YROWS = 3 * RD + 3 * RV // 2
-DT, VT = 3 * RD // 8, 3 * RV // 8
+YROWS = DR + VR // 2
+DT, VT = DR // 8, VR // 8
 SLOTS = SZ // KEEP
-PER = KEEP // 2
-ZSLOTS = DT + (VT + PER - 1) // PER
-ZT = (ZSLOTS + SLOTS - 1) // SLOTS
+ZB = (DT + SLOTS - 1) // SLOTS
+FOLDS = 3
+FW = (CY + 2) // FOLDS * SZ
+ZV = up_to(FW, 128)
+ZW = ZB * LW + ZV
 TAIL = MOST * BIN
 
 
@@ -126,15 +129,15 @@
     vref[...] = jnp.zeros_like(vref)
     for x in range(CX + 2):
         for c in range(3):
-            dref[c * RD + H - 1 + x : c * RD + H + x, :] = nodes[x, c : c + 1, :]
-            vref[c * RV + x : c * RV + x + 1, :] = nodes[x, 3 + c : 4 + c, :]
+            dref[c * DS + H - 1 + x : c * DS + H + x, :] = nodes[x, c : c + 1, :]
+            vref[c * VS + x : c * VS + x + 1, :] = nodes[x, 3 + c : 4 + c, :]
     for c in range(3):
-        at = c * RD + H - 1
+        at = c * DS + H - 1
         xs_high[c * KEEP : (c + 1) * KEEP, :] = dref[at + CX + 2 - KEEP : at + CX + 2, XA:XB]
         xs_low[c * KEEP : (c + 1) * KEEP, :] = dref[at : at + KEEP, XA:XB]
         at = 3 * KEEP + 2 * c
-        xs_high[at : at + 2, :] = vref[c * RV + CX : c * RV + CX + 2, XA:XB]
-        xs_low[at : at + 2, :] = vref[c * RV : c * RV + 2, XA:XB]
+        xs_high[at : at + 2, :] = vref[c * VS + CX : c * VS + CX + 2, XA:XB]
+        xs_low[at : at + 2, :] = vref[c * VS : c * VS + 2, XA:XB]
 
 
 def only(has, value):
@@ -145,17 +148,17 @@
     low = only(has_low, from_low[...])
     high = only(has_high, from_high[...])
     for c in range(3):
-        dref[c * RD : c * RD + KEEP, XA:XB] += low[c * KEEP : (c + 1) * KEEP]
-        dref[c * RD + SX - KEEP : c * RD + SX, XA:XB] += high[c * KEEP : (c + 1) * KEEP]
+        dref[c * DS : c * DS + KEEP, XA:XB] += low[c * KEEP : (c + 1) * KEEP]
+        dref[c * DS + SX - KEEP : c * DS + SX, XA:XB] += high[c * KEEP : (c + 1) * KEEP]
         at = 3 * KEEP + 2 * c
-        vref[c * RV : c * RV + 2, XA:XB] += low[at : at + 2]
-        vref[c * RV + CX : c * RV + CX + 2, XA:XB] += high[at : at + 2]
-    half = 3 * RV // 2
+        vref[c * VS : c * VS + 2, XA:XB] += low[at : at + 2]
+        vref[c * VS + CX : c * VS + CX + 2, XA:XB] += high[at : at + 2]
+    half = VR // 2
     for ys, d0, v0 in ((ys_high, CY * SZ, (H - 1 + CY) * SZ), (ys_low, (H - 1) * SZ, (H - 1) * SZ)):
-        ys[: 3 * RD, :] = take(dref, d0, KEEP * SZ)
+        ys[:DR, :] = take(dref.at[:DR], d0, KEEP * SZ)
         near = take(vref, v0, 2 * SZ)
-        ys[3 * RD :, 0:128] = near[:half]
-        ys[3 * RD :, 128:256] = near[half:]
+        ys[DR:, 0:128] = near[:half]
+        ys[DR:, 128:256] = near[half:]
 
 
 def lane_z():
@@ -164,16 +167,13 @@
     return lane - SZ * y, y
 
 
-def slot_of(t):
-    if t < DT:
-        s, sub, width = t, 0, KEEP
-    else:
-        s, sub, width = DT + (t - DT) // PER, 2 * ((t - DT) % PER), 2
-    return s // SLOTS, (s % SLOTS) * KEEP + sub, width
-
-
-def tile_of(t, dref, vref):
-    return dref.at[8 * t : 8 * t + 8] if t < DT else vref.at[8 * (t - DT) : 8 * (t - DT) + 8]
+def in_slot(z, at, width):
+    return (z >= at) & (z < at + width)
+
+
+def spin(value, shift):
+    shift = shift % value.shape[1]
+    return pltpu.roll(value, shift, 1) if shift else value
 
 
 def add_y(dref, vref, from_low, from_high, has_low, has_high, zs_low, zs_high):
@@ -181,39 +181,50 @@
         (from_low, has_low, 0, (H - 1) * SZ),
         (from_high, has_high, (SY - KEEP) * SZ, (H - 1 + CY) * SZ),
     ):
-        put_add(dref, d0, KEEP * SZ, only(has, got[: 3 * RD, :]))
-        near = jnp.concatenate([got[3 * RD :, 0:128], got[3 * RD :, 128:256]], axis=0)
+        put_add(dref.at[:DR], d0, KEEP * SZ, only(has, got[:DR, :]))
+        near = jnp.concatenate([got[DR:, 0:128], got[DR:, 128:256]], axis=0)
         put_add(vref, v0, 2 * SZ, only(has, near))
     z, _ = lane_z()
+    short = z[:, :ZV]
     for zs, d0, v0 in ((zs_high, CZ, H - 1 + CZ), (zs_low, H - 1, H - 1)):
-        out = [None] * ZT
-        for t in range(DT + VT):
-            block, at, width = slot_of(t)
-            shift = (at - (d0 if t < DT else v0)) % LW
-            value = tile_of(t, dref, vref)[...]
-            if shift:
-                value = pltpu.roll(value, shift, 1)
-            value = jnp.where((z >= at) & (z < at + width), value, 0.0)
-            out[block] = value if out[block] is None else out[block] + value
-        for block in range(ZT):
-            zs[8 * block : 8 * block + 8, :] = out[block]
+        for block in range(ZB):
+            out = jnp.zeros((8, LW), jnp.float32)
+            for s in range(min(SLOTS, DT - block * SLOTS)):
+                r = 8 * (block * SLOTS + s)
+                value = spin(dref[r : r + 8, :], s * KEEP - d0)
+                out = jnp.where(in_slot(z, s * KEEP, KEEP), value, out)
+            zs[:, block * LW : (block + 1) * LW] = out
+        out = jnp.zeros((8, ZV), jnp.float32)
+        for t in range(VT):
+            for q in range(FOLDS):
+                at = 2 * (t * FOLDS + q)
+                value = take(vref.at[8 * t : 8 * t + 8], (H - 1) * SZ + q * FW + v0, FW)
+                value = spin(value, at)
+                out = jnp.where(in_slot(short, at, 2), value, out)
+        zs[:, ZB * LW :] = out
 
 
 def add_z(dref, vref, from_low, from_high, has_low, has_high):
     z, _ = lane_z()
+    short = z[:, :ZV]
+    lane = lax.broadcasted_iota(jnp.int32, (8, ZV), 1)
     for got, has, d0, v0 in (
         (from_low, has_low, 0, H - 1),
         (from_high, has_high, SZ - KEEP, H - 1 + CZ),
     ):
-        for t in range(DT + VT):
-            block, at, width = slot_of(t)
-            value = only(has, got[8 * block : 8 * block + 8, :])
-            value = jnp.where((z >= at) & (z < at + width), value, 0.0)
-            shift = ((d0 if t < DT else v0) - at) % LW
-            if shift:
-                value = pltpu.roll(value, shift, 1)
-            tile = tile_of(t, dref, vref)
-            tile[...] += value
+        for block in range(ZB):
+            whole = only(has, got[:, block * LW : (block + 1) * LW])
+            for s in range(min(SLOTS, DT - block * SLOTS)):
+                r = 8 * (block * SLOTS + s)
+                value = jnp.where(in_slot(z, s * KEEP, KEEP), whole, 0.0)
+                dref[r : r + 8, :] += spin(value, d0 - s * KEEP)
+        whole = only(has, got[:, ZB * LW :])
+        for t in range(VT):
+            for q in range(FOLDS):
+                at = 2 * (t * FOLDS + q)
+                value = jnp.where(in_slot(short, at, 2) & (lane < FW), whole, 0.0)
+                value = spin(value, -at)
+                put_add(vref.at[8 * t : 8 * t + 8], (H - 1) * SZ + q * FW + v0, FW, value)
 
 
 def relax_all(dref, vref, place, nodes_x, nodes_y, nodes_z, wet, fields, field_left, damage_out):
@@ -228,8 +239,8 @@
     row_in = (gx >= 0) & (gx < nodes_x) & (row < SX)
     inside = row_in.astype(jnp.float32) * flat_in.astype(jnp.float32)
     mass = jnp.maximum(dref[0:RD, :], mass_floor)
-    damage = dref[RD : 2 * RD, :] / mass * inside
-    drive = dref[2 * RD : 3 * RD, :] / mass
+    damage = dref[DS : DS + RD, :] / mass * inside
+    drive = dref[2 * DS : 2 * DS + RD, :] / mass
     wet[0:RD, :] = mass
     wet[RD : 2 * RD, :] = inside
     for _ in range(SUBSTEPS):
@@ -249,7 +260,7 @@
     factor = wet[RD + H - 1 : RD + H - 1 + n, :] / wet[H - 1 : H - 1 + n, :]
     fields[...] = jnp.zeros_like(fields)
     for c in range(3):
-        fields[c * 16 : c * 16 + n, :] = vref[c * RV : c * RV + n, :] * factor
+        fields[c * 16 : c * 16 + n, :] = vref[c * VS : c * VS + n, :] * factor
     fields[48 : 48 + n, :] = wet[2 * RD + H - 1 : 2 * RD + H - 1 + n, :]
     whole = fields[...]
     for bc in range(4):
@@ -262,6 +273,7 @@
 
 def advance(part, base_ref, weight, slope, hot, field_left, out, at, count):
     lanes = slice(at, at + count)
+    there = slice(TAIL + at, TAIL + at + count)
     n = CX + 2
     high, low = split(field_left[...])
     got = jnp.dot(high, hot[:, lanes], preferred_element_type=jnp.float32)
@@ -301,9 +313,9 @@
     swell = bulk_coef * (jacobian - 1.0)
 
     def put(r, value):
-        out[r : r + 1, lanes] = value
-
-    out[0:2, lanes] = part[0:2, lanes]
+        out[r : r + 1, there] = value
+
+    out[0:2, there] = part[0:2, lanes]
     for i in range(3):
         put(2 + i, moved[i])
         put(25 + i, p(25 + i) + time_step * moved[i])
@@ -319,9 +331,9 @@
 
 
 def step_kernel(
-    sizes, part, base_ref, weight, slope, counts, updated, tail, damage_out,
+    sizes, part, base_ref, weight, slope, counts, migrated, damage_out,
     hot, coef, left, nodes, dref, vref, wet, fields, field_left,
-    sx, rx, sy, ry, sz, rz, give, take_in, send_sem, recv_sem,
+    sx, rx, sy, ry, sz, rz, ext, tell, told, send_sem, recv_sem,
 ):
     names = ("gx", "gy", "gz")
     place = [lax.axis_index(a) for a in names]
@@ -376,16 +388,34 @@
     add_z(dref, vref, rz.at[0], rz.at[1], has_low[2], has_high[2])
     relax_all(dref, vref, place, sizes[0] * CX, sizes[1] * CY, sizes[2] * CZ, wet, fields, field_left, damage_out)
     count = part.shape[1]
-    advance(part, base_ref, weight, slope, hot, field_left, updated, count - TAIL, TAIL)
-    give[0:28, :] = updated[:, count - TAIL :]
-    give[28:32, :] = jnp.broadcast_to(counts[0].astype(jnp.float32), (4, TAIL))
-    pass_on = pltpu.make_async_remote_copy(
-        src_ref=give, dst_ref=take_in, send_sem=send_sem.at[3, 0], recv_sem=recv_sem.at[3, 0],
-        device_id={"gz": following}, device_id_type=MESH)
-    pass_on.start()
-    advance(part, base_ref, weight, slope, hot, field_left, updated, 0, count - TAIL)
-    pass_on.wait()
-    tail[...] = take_in[...]
+
+    def to_next(src, dst, slot):
+        copy = pltpu.make_async_remote_copy(
+            src_ref=src, dst_ref=dst, send_sem=send_sem.at[3 + slot, 0], recv_sem=recv_sem.at[3 + slot, 0],
+            device_id={"gz": following}, device_id_type=MESH)
+        copy.start()
+        return copy
+
+    tell[...] = jnp.broadcast_to(counts[0], tell.shape)
+    flying = [to_next(tell, told, 0)]
+    chunk = TAIL // 2
+    for k in (1, 0):
+        at = count - TAIL + k * chunk
+        advance(part, base_ref, weight, slope, hot, field_left, ext, at, chunk)
+        flying.append(to_next(ext.at[:, TAIL + at : TAIL + at + chunk], ext.at[:, k * chunk : (k + 1) * chunk], 1 + k))
+    for at in range(0, count - TAIL, chunk):
+        advance(part, base_ref, weight, slope, hot, field_left, ext, at, min(chunk, count - TAIL - at))
+    ext[:, TAIL + count :] = jnp.zeros((28, TAIL), jnp.float32)
+    for copy in flying:
+        copy.wait()
+    prior = jnp.broadcast_to(told[0:1, :], (28, BIN))
+    live = prior + jnp.broadcast_to(count // BIN - counts[0], prior.shape)
+    block = lambda j: ext[:, j * BIN : (j + 1) * BIN]
+    for j in range(count // BIN + MOST):
+        piece = block(MOST + j)
+        for p in range(1, MOST + 1):
+            piece = jnp.where(prior == p, block(MOST - p + j), piece)
+        migrated[:, j * BIN : (j + 1) * BIN] = jnp.where(live > j, piece, 0.0)
 
 
 def per_device(particles, stencil_base, weights, gradients, counts):
@@ -393,23 +423,22 @@
     sizes = tuple(lax.axis_size(a) for a in ("gx", "gy", "gz"))
     vmem = pl.BlockSpec(memory_space=pltpu.VMEM)
     f32 = jnp.float32
-    updated, tail, flat_damage = pl.pallas_call(
+    migrated, flat_damage = pl.pallas_call(
         functools.partial(step_kernel, sizes),
         name="step",
         out_shape=(
-            jax.ShapeDtypeStruct((28, count), f32),
-            jax.ShapeDtypeStruct((32, TAIL), f32),
+            jax.ShapeDtypeStruct((28, count + TAIL), f32),
             jax.ShapeDtypeStruct((CX, LW), f32),
         ),
         in_specs=[vmem] * 4 + [pl.BlockSpec(memory_space=pltpu.SMEM)],
-        out_specs=(vmem,) * 3,
+        out_specs=(vmem,) * 2,
         scratch_shapes=[
             pltpu.VMEM((NB, count), jnp.bfloat16),
             pltpu.VMEM((32, count), f32),
             pltpu.VMEM(((CX + 2) * 64, count), jnp.bfloat16),
             pltpu.VMEM((CX + 2, 8, LW), f32),
-            pltpu.VMEM((3 * RD, LW), f32),
-            pltpu.VMEM((3 * RV, LW), f32),
+            pltpu.VMEM((up_to(2 * DS + RD, 8), LW), f32),
+            pltpu.VMEM((VR, LW), f32),
             pltpu.VMEM((3 * RD, LW), f32),
             pltpu.VMEM((64, LW), f32),
             pltpu.VMEM(((CX + 2) * 16, NB), f32),
@@ -417,26 +446,19 @@
             pltpu.VMEM((2, XROWS, XB - XA), f32),
             pltpu.VMEM((2, YROWS, YW), f32),
             pltpu.VMEM((2, YROWS, YW), f32),
-            pltpu.VMEM((2, 8 * ZT, LW), f32),
-            pltpu.VMEM((2, 8 * ZT, LW), f32),
-            pltpu.VMEM((32, TAIL), f32),
-            pltpu.VMEM((32, TAIL), f32),
-            pltpu.SemaphoreType.DMA((4, 2)),
-            pltpu.SemaphoreType.DMA((4, 2)),
+            pltpu.VMEM((2, 8, ZW), f32),
+            pltpu.VMEM((2, 8, ZW), f32),
+            pltpu.VMEM((28, count + 2 * TAIL), f32),
+            pltpu.VMEM((8, 128), jnp.int32),
+            pltpu.VMEM((8, 128), jnp.int32),
+            pltpu.SemaphoreType.DMA((6, 2)),
+            pltpu.SemaphoreType.DMA((6, 2)),
         ],
         compiler_params=pltpu.CompilerParams(
             collective_id=0, has_side_effects=True, vmem_limit_bytes=60 * 1024 * 1024
         ),
     )(particles, stencil_base, weights, gradients.reshape(24, count), counts)
     damage = flat_damage[:, : SY * SZ].reshape(CX, SY, SZ)[:, H : H + CY, H : H + CZ]
-    prior = tail[28, 0].astype(jnp.int32)
-    own_count = counts[0]
-    buffer_all = jnp.concatenate([tail[:28], updated, jnp.zeros((28, TAIL), f32)], axis=1)
-    start = (MOST - prior) * BIN
-    window = lax.dynamic_slice_in_dim(buffer_all, start, (NBIN + MOST) * BIN, 1)
-    live = (NBIN - own_count + prior) * BIN
-    slot = jnp.arange((NBIN + MOST) * BIN, dtype=jnp.int32)
-    migrated = jnp.where(slot[None, :] < live, window, jnp.zeros_like(window))
     return (migrated, damage)
 
 

time: 31.6 us -> 28.9 us (0.915)
  other arithmetic: 1.82 us -> 0 us
  Pallas kernels: 25.5 us -> 24 us
  local copies, waits for them, and re-layouts: 2.15 us -> 3.4 us
  between operations: 1.98 us -> 1.29 us
    select_n x1 -> x0, other arithmetic: 1.81 us -> none  [per_device(): migrated = jnp.where(slot[None, :] < live, window, jnp.zeros_like(window))]
    unnamed x2 -> x1, local copies, waits for them, and re-layouts: 0.01 us -> 1.77 us
    pallas_call x1, Pallas kernels: 25.5 us -> 24 us  [per_device(): pl.pallas_call(functools.partial(step_kernel, sizes), name='step', out_sh...]
    slice x1 -> x0, local copies, waits for them, and re-layouts: 1.19 us -> none  [per_device(): prior = tail[28, 0].astype(jnp.int32)]
    reshape x1, local copies, waits for them, and re-layouts: 0.15 us -> 0.92 us  [per_device(): damage = flat_damage[:, :SY * SZ].reshape(CX, SY, SZ)[:, H:H + CY, H:H + CZ]]
where the time goes in v2:
time: 28.9 us; the launch traced here: 28.7 us
  Pallas kernels  24 us (83%)
  local copies, waits for them, and re-layouts  3.4 us (12%)
  between operations  1.29 us (4%)
    pallas_call x1, Pallas kernels, per_device(): pl.pallas_call(functools.partial(step_kernel, sizes), name='step', out_sh...  24 us
    unnamed x1, local copies, waits for them, and re-layouts  1.77 us
    reshape x1, local copies, waits for them, and re-layouts, per_device(): damage = flat_damage[:, :SY * SZ].reshape(CX, SY, SZ)[:, H:H + CY, H:H + CZ]  0.92 us
    slice x1, local copies, waits for them, and re-layouts, per_device(): damage = flat_damage[:, :SY * SZ].reshape(CX, SY, SZ)[:, H:H + CY, H:H + CZ]  0.72 us

profile of v2, /device:TPU:0, one launch (start us, length us, event | category | flops | bytes accessed | tf_op | source)
XLA Modules:
  0.0 28.7 jit_solution(10757586679575779244)
XLA Ops:
  1.3 24.0 %step.1 = (f32[28,3072]{1,0:T(8,128)}, f32[8,1152]{1,0:T(8,128)}) custom-call(f32[28,2048]{1,0:T(8,128)} %part.1, s32[3,2048]{1,0:T(4,128)} %base_ref.1, f32[8,2048]{1,0:T(8,128)} %weight.1, f32[24,2048]{1,0:T(8,128)} %bitcast.2, s32[1]{0:T(128)S(6)} %copy.8.counts), custom_call_target="tpu_custom_call" | custom-call | tf_op jit(solution)/shard_map/step/pallas_call | solution.py:426
  25.2 0.9 %reshape.11 = f32[8,26,42]{2,1,0:T(8,128)S(1)} reshape(f32[8,1092]{1,0:T(8,128)} %bitcast.3) | data formatting | bytes 69888 | tf_op jit(solution)/shard_map/reshape | solution.py:461
  26.2 0.7 %slice.8 = f32[8,16,32]{2,1,0:T(8,128)} slice(f32[8,26,42]{2,1,0:T(8,128)S(1)} %reshape.11), slice={[0:8], [5:21], [5:37]} | slice | bytes 32768 | tf_op jit(solution)/shard_map/slice | solution.py:461
  26.9 1.8 %copy.9 = f32[28,3072]{1,0:T(8,128)} copy(f32[28,3072]{1,0:T(8,128)} %get-tuple-element.8) | data formatting | bytes 688128
